TPU v7x, 32 devices: a whole 2x2x4 slice. The times are simulated.
32 devices in a mesh: rows: 16 (over z, y, x), cols: 2 (over core).
Axes of the slice: x: 2, y: 2, z: 4, core: 2. Of those that a mesh axis runs over, the one named last changes fastest.
Arguments:
- row_points: float32 [3, 8192], P(None, 'rows')
- panel_points: bfloat16 [3, 512], P(None, ('rows', 'cols')), may hold values from 0 to 1
- test_vectors: bfloat16 [128, 512], P(None, ('rows', 'cols')), may hold values from -0.25 to 0.25
- leaf_skeleton: int32 [16, 64], P('rows'), may hold values from 0 to 511, as said below
- node_skeleton: int32 [16, 4, 64], P('rows'), may hold values from 0 to 127, as said below
Outputs:
- leaf_interp: float32 [64, 8192], P(None, ('rows', 'cols'))
- transfers: float32 [16, 4, 64, 128], P('rows')
- top_skeleton: float32 [16, 64, 256], P('rows')
Inputs may be any that keep to these rules, and one draw needn't show every extreme that they name: `leaf_skeleton`: each leaf's 64 entries are distinct. `node_skeleton`: each entry list holds 64 distinct positions among the 128 stacked rows (the lower child's first); all leaves under the same node have the same list at that level.
All inputs are finite; a program needn't handle non-finite values.
Results may differ from a plain program's by a relative error of at most 0.0049.
Values may be sent and summed in bfloat16 or wider, within the bound.
No kernel may reach another device: no remote copies, remote signals or barrier semaphores. Data moves between devices by JAX's collectives and lax.ppermute only.
A program may use at most 64 MiB of HBM per device.

v0:
```python
import math
import jax
import jax.numpy as jnp
from jax import lax
from jax.sharding import PartitionSpec as P

KAPPA = 40.0
SMOOTH = 0.05
RIDGE = 0.1
EPSILON = 1e-05


def from_partner(shard, axis, bit):
    return lax.ppermute(shard, axis, [(i, i ^ 1 << bit) for i in range(lax.axis_size(axis))])


def kernel_block(targets, sources):
    source_f = sources.astype(jnp.float32)
    dist_sq = jnp.zeros((targets.shape[1], source_f.shape[1]), jnp.float32)
    for component in range(3):
        offset = targets[component][:, None] - source_f[component][None, :]
        dist_sq = dist_sq + offset * offset
    radius = jnp.sqrt(dist_sq + SMOOTH * SMOOTH)
    real_part = (jnp.cos(KAPPA * radius) / radius).astype(jnp.bfloat16)
    imag_part = (jnp.sin(KAPPA * radius) / radius).astype(jnp.bfloat16)
    return (real_part, imag_part)


def sample_block(real_part, imag_part, vectors):
    first_half = jnp.dot(real_part, vectors.T, preferred_element_type=jnp.float32)
    second_half = jnp.dot(imag_part, vectors.T, preferred_element_type=jnp.float32)
    return jnp.concatenate([first_half, second_half], axis=1)


def interpolate(block, skeleton):
    gram_matrix = jnp.dot(skeleton, skeleton.T, precision=lax.Precision.HIGHEST)
    ridge = RIDGE * skeleton.shape[1] * (jnp.mean(skeleton * skeleton) + EPSILON)
    gram_matrix = gram_matrix + ridge * jnp.eye(skeleton.shape[0], dtype=jnp.float32)
    factor = jnp.linalg.cholesky(gram_matrix)
    right_side = jnp.dot(skeleton, block.T, precision=lax.Precision.HIGHEST)
    middle = lax.linalg.triangular_solve(factor, right_side, left_side=True, lower=True)
    return lax.linalg.triangular_solve(factor, middle, left_side=True, lower=True, transpose_a=True)


def body(row_points, panel_points, test_vectors, leaf_skeleton, node_skeleton):
    rows_here = row_points.shape[1]
    vec_count = test_vectors.shape[0]
    level_count = node_skeleton.shape[1]
    zero_sum = jnp.zeros((rows_here, 2 * vec_count), jnp.float32)
    running = zero_sum
    vectors = lax.all_gather(test_vectors, "rows", axis=1, tiled=True)
    sources = lax.all_gather(panel_points, "rows", axis=1, tiled=True)
    piece_width = vectors.shape[1]
    block_width = math.gcd(piece_width, 512)
    block_count = piece_width // block_width
    vec_blocks = jnp.moveaxis(vectors.reshape(vec_count, block_count, block_width), 1, 0)
    src_blocks = jnp.moveaxis(sources.reshape(3, block_count, block_width), 1, 0)

    def one_block(acc_sum, blocks):
        real_part, imag_part = kernel_block(row_points, blocks[1])
        return (acc_sum + sample_block(real_part, imag_part, blocks[0]), None)

    running, unused = lax.scan(one_block, running, (vec_blocks, src_blocks))
    half_rows = rows_here // lax.axis_size("cols")
    col_index = lax.axis_index("cols")
    samples = lax.psum(running, "cols")
    skel_rows = jnp.take(samples, leaf_skeleton[0], axis=0)
    own_samples = lax.dynamic_slice_in_dim(samples, col_index * half_rows, half_rows, 0)
    leaf_interp = interpolate(own_samples, skel_rows)
    row_index = lax.axis_index("rows")
    current = skel_rows
    level_maps = []
    for tree_level in range(level_count):
        partner = from_partner(current, "rows", tree_level)
        is_upper = jnp.right_shift(row_index, tree_level) & 1 == 1
        lower_child = jnp.where(is_upper, partner, current)
        upper_child = jnp.where(is_upper, current, partner)
        stacked = jnp.concatenate([lower_child, upper_child], axis=0)
        current = jnp.take(stacked, node_skeleton[0, tree_level], axis=0)
        level_maps.append(interpolate(stacked, current))
    path_maps = jnp.stack(level_maps)
    return (leaf_interp, path_maps[None], current[None])


def solution(mesh):
    placed = (
        P(None, "rows"),
        P(None, ("rows", "cols")),
        P(None, ("rows", "cols")),
        P("rows", None),
        P("rows", None, None),
    )
    return jax.shard_map(
        body,
        mesh=mesh,
        in_specs=placed,
        out_specs=(P(None, ("rows", "cols")), P("rows", None, None, None), P("rows", None, None)),
        check_vma=False,
    )
```

profile of v0, /device:TPU:0, one launch (start us, length us, event | category | flops | bytes accessed | tf_op | source)
XLA Modules:
  0.0 203.0 jit_solution(5670295947467593674)
XLA Ops:
  7.2 0.6 copy-done.4
  7.8 42.5 %all-gather = bf16[16,16,3]{1,2,0:T(4,128)(2,1)S(1)} all-gather(bf16[1,16,3]{1,2,0:T(4,128)(2,1)S(1)} %bitcast.136), channel_id=1, replica_groups=mesh['rows'=16,'cols'=2] {'rows'}, dimensions={0}, use_global_device_ids=true | all-gather | bytes 1632 | tf_op jit(solution)/shard_map/all_gather | solution.py:52
  50.4 0.6 copy-done.1
  51.0 0.7 copy-done.2
  51.7 35.8 %all_gather.7 = bf16[128,256]{0,1:T(8,128)(2,1)S(1)} all-gather(bf16[128,16]{0,1:T(8,128)(2,1)S(1)} %copy-done.2), channel_id=1, replica_groups=mesh['rows'=16,'cols'=2] {'rows'}, dimensions={1}, use_global_device_ids=true | all-gather | bytes 69632 | tf_op jit(solution)/shard_map/all_gather | solution.py:51
  87.5 2.4 %fusion = f32[512,128]{0,1:T(8,128)S(1)} fusion(bf16[128,256]{0,1:T(8,128)(2,1)S(1)} %all_gather.7, f32[256]{0:T(256)S(1)} %bitcast.139, f32[512]{0:T(512)S(1)} %bitcast.132, f32[256]{0:T(256)S(1)} %bitcast.141, f32[512]{0:T(512)S(1)} %bitcast.134, f32[256]{0:T(256)S(1)} %bitcast.137, f32[512]{0:T(512)S(1)} %bitcast.130), kind=kOutput, calls=%fused_computation.18 | convolution fusion | flops 35127296 | bytes 336896 | tf_op jit(solution)/shard_map/while/body/eval_jaxpr/dot_general | solution.py:30
  89.9 2.4 %fusion.1 = f32[512,128]{0,1:T(8,128)S(1)} fusion(bf16[128,256]{0,1:T(8,128)(2,1)S(1)} %all_gather.7, f32[256]{0:T(256)S(1)} %bitcast.140, f32[512]{0:T(512)S(1)} %bitcast.133, f32[256]{0:T(256)S(1)} %bitcast.142, f32[512]{0:T(512)S(1)} %bitcast.135, f32[256]{0:T(256)S(1)} %bitcast.138, f32[512]{0:T(512)S(1)} %bitcast.131), kind=kOutput, calls=%fused_computation.19 | convolution fusion | flops 35127296 | bytes 336896 | tf_op jit(solution)/shard_map/while/body/eval_jaxpr/dot_general | solution.py:31
  92.3 0.8 pad_maximum_fusion
  93.1 0.6 copy-done.5
  93.8 0.7 copy-done.3
  94.6 15.1 %all-reduce.2.cloned.1.call-done = f32[512,256]{0,1:T(8,128)} async-done(((f32[512,256]{0,1:T(8,128)}), f32[512,256]{0,1:T(8,128)}) %all-reduce.2.cloned.1.call-update) | async-done | bytes 524304 | tf_op jit(solution)/shard_map/psum | solution.py:66
  109.7 1.2 copy.53
  110.9 0.7 gather_fusion
  111.6 0.7 multiply_reduce_fusion.4
  112.3 1.8 collective-permute-start
  114.7 0.2 convolution_add_fusion.4
  115.0 5.8 %cholesky.89 = f32[64,64]{1,0:T(8,128)S(1)} custom-call(f32[64,64]{1,0:T(8,128)S(1)} %fusion.48), custom_call_target="Cholesky" | custom-call | tf_op jit(solution)/shard_map/jit(cholesky)/cholesky | solution.py:39
  121.0 0.6 compare_reduce_fusion.4
  121.7 0.7 fusion.23
  122.4 4.9 %custom-call.13 = f32[1,64,64]{1,2,0:T(8,128)S(1)} custom-call(f32[1,64,64]{2,1,0:T(8,128)S(1)} %copy.58), custom_call_target="InvertDiagBlocksLowerTriangular" | custom-call | tf_op jit(solution)/shard_map/triangular_solve | solution.py:42
  127.4 0.3 fusion.2
  127.6 0.3 fusion.46
  127.9 0.8 fusion.44
  128.8 0.7 gather_fusion.1
  129.4 0.7 multiply_reduce_fusion.3
  130.1 0.3 fusion.68
  130.4 1.5 collective-permute-start.1
  132.6 0.2 convolution_add_fusion.3
  132.9 5.8 %cholesky.100 = f32[64,64]{1,0:T(8,128)S(1)} custom-call(f32[64,64]{1,0:T(8,128)S(1)} %fusion.43), custom_call_target="Cholesky" | custom-call | tf_op jit(solution)/shard_map/jit(cholesky)/cholesky | solution.py:39
  138.7 0.6 compare_reduce_fusion.3
  139.4 0.7 fusion.24
  140.1 4.9 %custom-call.21 = f32[1,64,64]{1,2,0:T(8,128)S(1)} custom-call(f32[1,64,64]{2,1,0:T(8,128)S(1)} %fusion.24), custom_call_target="InvertDiagBlocksLowerTriangular" | custom-call | tf_op jit(solution)/shard_map/triangular_solve/custom-call.4 | solution.py:42
  144.9 0.3 fusion.40
  145.2 0.2 convolution_bitcast_fusion.3
  145.4 0.7 gather_fusion.2
  146.1 0.7 multiply_reduce_fusion.2
  146.8 0.3 fusion.67
  147.0 1.5 collective-permute-start.2
  149.2 0.2 convolution_add_fusion.2
  149.5 5.8 %cholesky.111 = f32[64,64]{1,0:T(8,128)S(1)} custom-call(f32[64,64]{1,0:T(8,128)S(1)} %fusion.39), custom_call_target="Cholesky" | custom-call | tf_op jit(solution)/shard_map/jit(cholesky)/cholesky | solution.py:39
  155.4 0.6 compare_reduce_fusion.2
  156.1 0.7 fusion.25
  156.7 4.9 %custom-call.23 = f32[1,64,64]{1,2,0:T(8,128)S(1)} custom-call(f32[1,64,64]{2,1,0:T(8,128)S(1)} %fusion.25), custom_call_target="InvertDiagBlocksLowerTriangular" | custom-call | tf_op jit(solution)/shard_map/triangular_solve/custom-call.4 | solution.py:42
  161.6 0.3 fusion.36
  162.1 0.7 gather_fusion.3
  162.8 0.7 multiply_reduce_fusion.1
  163.5 0.3 fusion.66
  163.7 2.5 %collective-permute-start.3 = (f32[64,256]{1,0:T(8,128)S(1)}, f32[64,256]{1,0:T(8,128)S(1)}, u32[]{:S(2)}, u32[]{:S(2)}) collective-permute-start(f32[64,256]{1,0:T(8,128)S(1)} %get-tuple-element.27), channel_id=1, source_target_pairs={{0,16},{2,18},{4,20},{6,22},{8,24},{10,26},{12,28},{14,30},{16,0},... | collective-permute-start | bytes 196616 | tf_op jit(solution)/shard_map/ppermute | solution.py:14
  166.8 0.2 convolution_add_fusion.1
  167.1 5.8 %cholesky.122 = f32[64,64]{1,0:T(8,128)S(1)} custom-call(f32[64,64]{1,0:T(8,128)S(1)} %fusion.35), custom_call_target="Cholesky" | custom-call | tf_op jit(solution)/shard_map/jit(cholesky)/cholesky | solution.py:39
  173.0 0.6 compare_reduce_fusion.1
  173.7 0.7 fusion.26
  174.3 4.9 %custom-call.25 = f32[1,64,64]{1,2,0:T(8,128)S(1)} custom-call(f32[1,64,64]{2,1,0:T(8,128)S(1)} %fusion.26), custom_call_target="InvertDiagBlocksLowerTriangular" | custom-call | tf_op jit(solution)/shard_map/triangular_solve/custom-call.4 | solution.py:42
  179.2 0.3 fusion.32
  179.7 0.7 gather_fusion.4
  180.4 1.3 select_bitcast_fusion
  181.7 0.3 fusion.20
  182.6 0.3 convolution_add_fusion
  183.0 5.8 %cholesky.133 = f32[64,64]{1,0:T(8,128)S(1)} custom-call(f32[64,64]{1,0:T(8,128)S(1)} %fusion.31), custom_call_target="Cholesky" | custom-call | tf_op jit(solution)/shard_map/jit(cholesky)/cholesky | solution.py:39
  188.9 0.6 compare_reduce_fusion
  189.5 0.7 fusion.27
  190.2 4.9 %custom-call.27 = f32[1,64,64]{1,2,0:T(8,128)S(1)} custom-call(f32[1,64,64]{2,1,0:T(8,128)S(1)} %fusion.27), custom_call_target="InvertDiagBlocksLowerTriangular" | custom-call | tf_op jit(solution)/shard_map/triangular_solve/custom-call.4 | solution.py:42
  195.1 0.3 fusion.28
  195.5 0.7 maximum_bitcast_fusion
  (53 shorter events, 1.6 us)
Async XLA Ops:
  7.2 0.7 copy-start.4
  7.2 102.5 %all-reduce.2.cloned.1.call-start = ((), (), s32[]{:S(2)}) async-start(), calls=%async_computation | async-start | bytes 1048576 | tf_op jit(solution)/shard_map/psum | solution.py:66
  50.3 0.7 copy-start.1
  51.0 0.7 copy-start.2
  93.1 0.7 copy-start.5
  93.8 0.7 copy-start.3
  110.9 16.4 %copy-start = (f32[512,256]{0,1:T(8,128)S(1)}, f32[512,256]{0,1:T(8,128)}, u32[]{:S(2)}) copy-start(f32[512,256]{0,1:T(8,128)} %all-reduce.2.cloned.1.call-done) | copy-start | bytes 1572868
  112.3 16.5 %collective-permute-start = (f32[64,256]{1,0:T(8,128)S(1)}, f32[64,256]{1,0:T(8,128)S(1)}, u32[]{:S(2)}, u32[]{:S(2)}) collective-permute-start(f32[64,256]{1,0:T(8,128)S(1)} %get-tuple-element.37), channel_id=1, source_target_pairs={{0,2},{2,0},{4,6},{6,4},{8,10},{10,8},{12,14},{14,12},{16,18},{18,... | collective-permute-start | bytes 196616 | tf_op jit(solution)/shard_map/ppermute | solution.py:14
  130.4 15.0 %collective-permute-start.1 = (f32[64,256]{1,0:T(8,128)S(1)}, f32[64,256]{1,0:T(8,128)S(1)}, u32[]{:S(2)}, u32[]{:S(2)}) collective-permute-start(f32[64,256]{1,0:T(8,128)S(1)} %get-tuple-element.23), channel_id=1, source_target_pairs={{0,4},{2,6},{4,0},{6,2},{8,12},{10,14},{12,8},{14,10},{16,20},{18,... | collective-permute-start | bytes 196616 | tf_op jit(solution)/shard_map/ppermute | solution.py:14
  147.0 15.0 %collective-permute-start.2 = (f32[64,256]{1,0:T(8,128)S(1)}, f32[64,256]{1,0:T(8,128)S(1)}, u32[]{:S(2)}, u32[]{:S(2)}) collective-permute-start(f32[64,256]{1,0:T(8,128)S(1)} %get-tuple-element.25), channel_id=1, source_target_pairs={{0,8},{2,10},{4,12},{6,14},{8,0},{10,2},{12,4},{14,6},{16,24},{18,... | collective-permute-start | bytes 196616 | tf_op jit(solution)/shard_map/ppermute | solution.py:14
  163.7 15.9 %collective-permute-start.3 = (f32[64,256]{1,0:T(8,128)S(1)}, f32[64,256]{1,0:T(8,128)S(1)}, u32[]{:S(2)}, u32[]{:S(2)}) collective-permute-start(f32[64,256]{1,0:T(8,128)S(1)} %get-tuple-element.27), channel_id=1, source_target_pairs={{0,16},{2,18},{4,20},{6,22},{8,24},{10,26},{12,28},{14,30},{16,0},... | collective-permute-start | bytes 196616 | tf_op jit(solution)/shard_map/ppermute | solution.py:14
Sparse Core Ops, SparseCore 0:
  93.3 16.3 all-reduce.1
where the time goes:
time: 203 us
  blocking collectives  78.3 us (39%)
  other arithmetic  66.2 us (33%)
  between operations  17.8 us (9%)
  waiting for transfers between devices  15.1 us (7%)
  matrix products  9.95 us (5%)
  local copies, waits for them, and re-layouts  8.37 us (4%)
  starting transfers between devices  7.37 us (4%)
    all_gather x1, blocking collectives, body(): sources = lax.all_gather(panel_points, 'rows', axis=1, tiled=True)  42.5 us
    all_gather x1, blocking collectives, body(): vectors = lax.all_gather(test_vectors, 'rows', axis=1, tiled=True)  35.8 us
    another operation x15, other arithmetic, interpolate(): factor = jnp.linalg.cholesky(gram_matrix)  32.7 us
    another operation x10, other arithmetic, interpolate(): lax.linalg.triangular_solve(factor, middle, left_side=True, lower=True, t...  27.8 us
    psum x1, waiting for transfers between devices, body(): samples = lax.psum(running, 'cols')  15.1 us
    ppermute x4, starting transfers between devices, from_partner(): lax.ppermute(shard, axis, [(i, i ^ 1 << bit) for i in range(lax.axis_size...  7.33 us
  transfers between devices with their start and end apart: 5, of which 1 were waited for; matrix products, arithmetic and copies ran while one was open for 26% of the time, Pallas kernels for 0%

commit v1 on v0

--- a/solution.py
+++ b/solution.py
@@ -8,6 +8,23 @@
 SMOOTH = 0.05
 RIDGE = 0.1
 EPSILON = 1e-05
+
+
+def joined_along(pieces, dim):
+    pieces = jnp.moveaxis(pieces, 0, dim)
+    lengths = pieces.shape
+    return pieces.reshape(*lengths[:dim], lengths[dim] * lengths[dim + 1], *lengths[dim + 2 :])
+
+
+def grow_blocks(x, axis):
+    peers, position = (lax.axis_size(axis), lax.axis_index(axis))
+    blocks, bit = (x[None], 1)
+    while bit < peers:
+        other = lax.ppermute(blocks, axis, [(i, i ^ bit) for i in range(peers)])
+        low = position & bit == 0
+        blocks = jnp.concatenate([jnp.where(low, blocks, other), jnp.where(low, other, blocks)])
+        bit *= 2
+    return blocks
 
 
 def from_partner(shard, axis, bit):
@@ -48,7 +65,7 @@
     level_count = node_skeleton.shape[1]
     zero_sum = jnp.zeros((rows_here, 2 * vec_count), jnp.float32)
     running = zero_sum
-    vectors = lax.all_gather(test_vectors, "rows", axis=1, tiled=True)
+    vectors = joined_along(grow_blocks(test_vectors, "rows"), 1)
     sources = lax.all_gather(panel_points, "rows", axis=1, tiled=True)
     piece_width = vectors.shape[1]
     block_width = math.gcd(piece_width, 512)

time: 203 us -> 179 us (0.88)
  blocking collectives: 78.3 us -> 40.1 us
  waiting for transfers between devices: 15.1 us -> 26.1 us
  starting transfers between devices: 7.37 us -> 10.6 us
    all_gather x1 -> x0, blocking collectives: 35.8 us -> none  [body(): vectors = lax.all_gather(test_vectors, 'rows', axis=1, tiled=True)]
    ppermute x0 -> x4, waiting for transfers between devices: none -> 11.5 us  [grow_blocks(): other = lax.ppermute(blocks, axis, [(i, i ^ bit) for i in range(peers)])]
    ppermute x0 -> x4, starting transfers between devices: none -> 3.24 us  [grow_blocks(): other = lax.ppermute(blocks, axis, [(i, i ^ bit) for i in range(peers)])]
    all_gather x1, blocking collectives: 42.5 us -> 40.1 us  [body(): sources = lax.all_gather(panel_points, 'rows', axis=1, tiled=True)]
  transfers between devices with their start and end apart: 5 -> 9, of which waited for: 1 -> 4; matrix products, arithmetic and copies ran while one was open for 26% -> 29% of each run, Pallas kernels for 0% -> 0%
where the time goes in v1:
time: 179 us
  other arithmetic  66.4 us (37%)
  blocking collectives  40.1 us (22%)
  waiting for transfers between devices  26.1 us (15%)
  between operations  17.8 us (10%)
  starting transfers between devices  10.6 us (6%)
  matrix products  9.95 us (6%)
  local copies, waits for them, and re-layouts  7.66 us (4%)
    all_gather x1, blocking collectives, body(): sources = lax.all_gather(panel_points, 'rows', axis=1, tiled=True)  40.1 us
    another operation x15, other arithmetic, interpolate(): factor = jnp.linalg.cholesky(gram_matrix)  32.8 us
    another operation x10, other arithmetic, interpolate(): lax.linalg.triangular_solve(factor, middle, left_side=True, lower=True, t...  27.8 us
    psum x1, waiting for transfers between devices, body(): samples = lax.psum(running, 'cols')  14.6 us
    ppermute x4, waiting for transfers between devices, grow_blocks(): other = lax.ppermute(blocks, axis, [(i, i ^ bit) for i in range(peers)])  11.5 us
    ppermute x4, starting transfers between devices, from_partner(): lax.ppermute(shard, axis, [(i, i ^ 1 << bit) for i in range(lax.axis_size...  7.32 us
  transfers between devices with their start and end apart: 9, of which 4 were waited for; matrix products, arithmetic and copies ran while one was open for 29% of the time, Pallas kernels for 0%

profile of v1, /device:TPU:0, one launch (start us, length us, event | category | flops | bytes accessed | tf_op | source)
XLA Modules:
  0.0 178.7 jit_solution(288993253536378134)
XLA Ops:
  7.2 3.0 %collective-permute-start = (bf16[1,128,16]{1,2,0:T(8,128)(2,1)}, bf16[1,128,16]{1,2,0:T(8,128)(2,1)S(1)}, u32[]{:S(2)}, u32[]{:S(2)}) collective-permute-start(bf16[1,128,16]{1,2,0:T(8,128)(2,1)} %bitcast.138), channel_id=1, source_target_pairs={{0,2},{2,0},{4,6},{6,4},{8,10},{10,8},{12,14},{14,12},{16,18},{18,... | collective-permute-start | bytes 12296 | tf_op jit(solution)/shard_map/ppermute | solution.py:23
  10.3 40.1 %all-gather = bf16[16,16,3]{1,2,0:T(4,128)(2,1)S(1)} all-gather(bf16[1,16,3]{1,2,0:T(4,128)(2,1)S(1)} %bitcast.145), channel_id=1, replica_groups=mesh['rows'=16,'cols'=2] {'rows'}, dimensions={0}, use_global_device_ids=true | all-gather | bytes 1632 | tf_op jit(solution)/shard_map/all_gather | solution.py:69
  50.5 0.6 copy-done.1
  51.1 0.7 copy-done.3
  51.8 0.7 copy-done.2
  52.5 0.6 copy-done.5
  53.1 3.1 %collective-permute-done.1 = bf16[2,128,16]{1,2,0:T(8,128)(2,1)S(1)} collective-permute-done((bf16[2,128,16]{1,2,0:T(8,128)(2,1)S(1)}, bf16[2,128,16]{1,2,0:T(8,128)(2,1)S(1)}, u32[]{:S(2)}, u32[]{:S(2)}) %collective-permute-start.1) | collective-permute-done | bytes 8224 | tf_op jit(solution)/shard_map/ppermute | solution.py:23
  56.3 3.7 %collective-permute-done.2 = bf16[4,128,16]{1,2,0:T(8,128)(2,1)S(1)} collective-permute-done((bf16[4,128,16]{1,2,0:T(8,128)(2,1)S(1)}, bf16[4,128,16]{1,2,0:T(8,128)(2,1)S(1)}, u32[]{:S(2)}, u32[]{:S(2)}) %collective-permute-start.2) | collective-permute-done | bytes 16416 | tf_op jit(solution)/shard_map/ppermute | solution.py:23
  60.1 4.8 %collective-permute-done.3 = bf16[8,128,16]{1,2,0:T(8,128)(2,1)S(1)} collective-permute-done((bf16[8,128,16]{1,2,0:T(8,128)(2,1)S(1)}, bf16[8,128,16]{1,2,0:T(8,128)(2,1)S(1)}, u32[]{:S(2)}, u32[]{:S(2)}) %collective-permute-start.3) | collective-permute-done | bytes 32800 | tf_op jit(solution)/shard_map/ppermute | solution.py:23
  64.9 2.4 %fusion = f32[512,128]{0,1:T(8,128)S(1)} fusion(bf16[128,256]{0,1:T(8,128)(2,1)S(1)} %bitcast.135, f32[256]{0:T(256)S(1)} %bitcast.148, f32[512]{0:T(512)S(1)} %bitcast.141, f32[256]{0:T(256)S(1)} %bitcast.150, f32[512]{0:T(512)S(1)} %bitcast.143, f32[256]{0:T(256)S(1)} %bitcast.146, f32[512]{0:T(512)S(1)} %bitcast.139), kind=kOutput, calls=%fused_computation.18 | convolution fusion | flops 35127296 | bytes 336896 | tf_op jit(solution)/shard_map/while/body/eval_jaxpr/dot_general | solution.py:47
  67.3 2.4 %fusion.1 = f32[512,128]{0,1:T(8,128)S(1)} fusion(bf16[128,256]{0,1:T(8,128)(2,1)S(1)} %bitcast.136, f32[256]{0:T(256)S(1)} %bitcast.149, f32[512]{0:T(512)S(1)} %bitcast.142, f32[256]{0:T(256)S(1)} %bitcast.151, f32[512]{0:T(512)S(1)} %bitcast.144, f32[256]{0:T(256)S(1)} %bitcast.147, f32[512]{0:T(512)S(1)} %bitcast.140), kind=kOutput, calls=%fused_computation.19 | convolution fusion | flops 35127296 | bytes 336896 | tf_op jit(solution)/shard_map/while/body/eval_jaxpr/dot_general | solution.py:48
  69.7 0.8 pad_maximum_fusion
  70.6 14.6 %all-reduce.2.cloned.1.call-done = f32[512,256]{0,1:T(8,128)} async-done(((f32[512,256]{0,1:T(8,128)}), f32[512,256]{0,1:T(8,128)}) %all-reduce.2.cloned.1.call-update) | async-done | bytes 524304 | tf_op jit(solution)/shard_map/psum | solution.py:83
  85.2 1.2 copy.53
  86.5 0.7 gather_fusion
  87.1 0.7 multiply_reduce_fusion.4
  87.8 1.8 collective-permute-start.4
  90.2 0.2 convolution_add_fusion.4
  90.5 5.8 %cholesky.89 = f32[64,64]{1,0:T(8,128)S(1)} custom-call(f32[64,64]{1,0:T(8,128)S(1)} %fusion.48), custom_call_target="Cholesky" | custom-call | tf_op jit(solution)/shard_map/jit(cholesky)/cholesky | solution.py:56
  96.6 0.6 compare_reduce_fusion.4
  97.2 0.7 fusion.23
  98.0 4.9 %custom-call.13 = f32[1,64,64]{1,2,0:T(8,128)S(1)} custom-call(f32[1,64,64]{2,1,0:T(8,128)S(1)} %copy.58), custom_call_target="InvertDiagBlocksLowerTriangular" | custom-call | tf_op jit(solution)/shard_map/triangular_solve | solution.py:59
  102.9 0.3 fusion.2
  103.2 0.3 fusion.46
  103.4 0.8 fusion.44
  104.3 0.7 gather_fusion.1
  105.0 0.7 multiply_reduce_fusion.3
  105.6 0.3 fusion.68
  105.9 1.5 collective-permute-start.5
  108.4 5.8 %cholesky.100 = f32[64,64]{1,0:T(8,128)S(1)} custom-call(f32[64,64]{1,0:T(8,128)S(1)} %fusion.43), custom_call_target="Cholesky" | custom-call | tf_op jit(solution)/shard_map/jit(cholesky)/cholesky | solution.py:56
  114.3 0.6 compare_reduce_fusion.3
  114.9 0.7 fusion.24
  115.6 4.9 %custom-call.21 = f32[1,64,64]{1,2,0:T(8,128)S(1)} custom-call(f32[1,64,64]{2,1,0:T(8,128)S(1)} %fusion.24), custom_call_target="InvertDiagBlocksLowerTriangular" | custom-call | tf_op jit(solution)/shard_map/triangular_solve/custom-call.4 | solution.py:59
  120.5 0.3 fusion.40
  121.0 0.7 gather_fusion.2
  121.6 0.7 multiply_reduce_fusion.2
  122.3 0.3 fusion.67
  122.6 1.5 collective-permute-start.6
  124.8 0.2 convolution_add_fusion.2
  125.1 6.0 %cholesky.111 = f32[64,64]{1,0:T(8,128)S(1)} custom-call(f32[64,64]{1,0:T(8,128)S(1)} %fusion.39), custom_call_target="Cholesky" | custom-call | tf_op jit(solution)/shard_map/jit(cholesky)/cholesky | solution.py:56
  131.1 0.6 compare_reduce_fusion.2
  131.7 0.7 fusion.25
  132.4 4.9 %custom-call.23 = f32[1,64,64]{1,2,0:T(8,128)S(1)} custom-call(f32[1,64,64]{2,1,0:T(8,128)S(1)} %fusion.25), custom_call_target="InvertDiagBlocksLowerTriangular" | custom-call | tf_op jit(solution)/shard_map/triangular_solve/custom-call.4 | solution.py:59
  137.3 0.3 fusion.36
  137.8 0.7 gather_fusion.3
  138.4 0.7 multiply_reduce_fusion.1
  139.1 0.3 fusion.66
  139.4 2.5 %collective-permute-start.7 = (f32[64,256]{1,0:T(8,128)S(1)}, f32[64,256]{1,0:T(8,128)S(1)}, u32[]{:S(2)}, u32[]{:S(2)}) collective-permute-start(f32[64,256]{1,0:T(8,128)S(1)} %get-tuple-element.27), channel_id=1, source_target_pairs={{0,16},{2,18},{4,20},{6,22},{8,24},{10,26},{12,28},{14,30},{16,0},... | collective-permute-start | bytes 196616 | tf_op jit(solution)/shard_map/ppermute | solution.py:31
  142.5 0.2 convolution_add_fusion.1
  142.8 5.8 %cholesky.122 = f32[64,64]{1,0:T(8,128)S(1)} custom-call(f32[64,64]{1,0:T(8,128)S(1)} %fusion.35), custom_call_target="Cholesky" | custom-call | tf_op jit(solution)/shard_map/jit(cholesky)/cholesky | solution.py:56
  148.7 0.6 compare_reduce_fusion.1
  149.3 0.7 fusion.26
  150.0 4.9 %custom-call.25 = f32[1,64,64]{1,2,0:T(8,128)S(1)} custom-call(f32[1,64,64]{2,1,0:T(8,128)S(1)} %fusion.26), custom_call_target="InvertDiagBlocksLowerTriangular" | custom-call | tf_op jit(solution)/shard_map/triangular_solve/custom-call.4 | solution.py:59
  154.9 0.3 fusion.32
  155.4 0.7 gather_fusion.4
  156.0 1.3 select_bitcast_fusion
  157.3 0.3 fusion.20
  158.3 0.3 convolution_add_fusion
  158.7 5.8 %cholesky.133 = f32[64,64]{1,0:T(8,128)S(1)} custom-call(f32[64,64]{1,0:T(8,128)S(1)} %fusion.31), custom_call_target="Cholesky" | custom-call | tf_op jit(solution)/shard_map/jit(cholesky)/cholesky | solution.py:56
  164.5 0.6 compare_reduce_fusion
  165.2 0.7 fusion.27
  165.8 4.9 %custom-call.27 = f32[1,64,64]{1,2,0:T(8,128)S(1)} custom-call(f32[1,64,64]{2,1,0:T(8,128)S(1)} %fusion.27), custom_call_target="InvertDiagBlocksLowerTriangular" | custom-call | tf_op jit(solution)/shard_map/triangular_solve/custom-call.4 | solution.py:59
  170.7 0.3 fusion.28
  171.2 0.7 maximum_bitcast_fusion
  (68 shorter events, 2.3 us)
Async XLA Ops:
  7.2 78.0 %all-reduce.2.cloned.1.call-start = ((), (), s32[]{:S(2)}) async-start(), calls=%async_computation | async-start | bytes 1048576 | tf_op jit(solution)/shard_map/psum | solution.py:83
  7.2 3.0 %copy-start.4 = (bf16[3,16]{1,0:T(4,128)(2,1)S(1)}, bf16[3,16]{1,0:T(4,128)(2,1)}, u32[]{:S(2)}) copy-start(bf16[3,16]{1,0:T(4,128)(2,1)} %param.13) | copy-start | bytes 292
  7.2 44.6 %collective-permute-start = (bf16[1,128,16]{1,2,0:T(8,128)(2,1)}, bf16[1,128,16]{1,2,0:T(8,128)(2,1)S(1)}, u32[]{:S(2)}, u32[]{:S(2)}) collective-permute-start(bf16[1,128,16]{1,2,0:T(8,128)(2,1)} %bitcast.138), channel_id=1, source_target_pairs={{0,2},{2,0},{4,6},{6,4},{8,10},{10,8},{12,14},{14,12},{16,18},{18,... | collective-permute-start | bytes 12296 | tf_op jit(solution)/shard_map/ppermute | solution.py:23
  50.4 0.7 copy-start.1
  51.1 0.7 copy-start.3
  51.8 0.7 copy-start.2
  52.5 0.7 copy-start.5
  52.5 3.7 %collective-permute-start.1 = (bf16[2,128,16]{1,2,0:T(8,128)(2,1)S(1)}, bf16[2,128,16]{1,2,0:T(8,128)(2,1)S(1)}, u32[]{:S(2)}, u32[]{:S(2)}) collective-permute-start(bf16[2,128,16]{1,2,0:T(8,128)(2,1)S(1)} %pad_maximum_fusion.8), channel_id=1, source_target_pairs={{0,4},{2,6},{4,0},{6,2},{8,12},{10,14},{12,8},{14,10},{16,20},{18,... | collective-permute-start | bytes 24584 | tf_op jit(solution)/shard_map/ppermute | solution.py:23
  56.2 3.8 %collective-permute-start.2 = (bf16[4,128,16]{1,2,0:T(8,128)(2,1)S(1)}, bf16[4,128,16]{1,2,0:T(8,128)(2,1)S(1)}, u32[]{:S(2)}, u32[]{:S(2)}) collective-permute-start(bf16[4,128,16]{1,2,0:T(8,128)(2,1)S(1)} %pad_maximum_fusion.7), channel_id=1, source_target_pairs={{0,8},{2,10},{4,12},{6,14},{8,0},{10,2},{12,4},{14,6},{16,24},{18,... | collective-permute-start | bytes 49160 | tf_op jit(solution)/shard_map/ppermute | solution.py:23
  60.0 4.9 %collective-permute-start.3 = (bf16[8,128,16]{1,2,0:T(8,128)(2,1)S(1)}, bf16[8,128,16]{1,2,0:T(8,128)(2,1)S(1)}, u32[]{:S(2)}, u32[]{:S(2)}) collective-permute-start(bf16[8,128,16]{1,2,0:T(8,128)(2,1)S(1)} %pad_maximum_fusion.6), channel_id=1, source_target_pairs={{0,16},{2,18},{4,20},{6,22},{8,24},{10,26},{12,28},{14,30},{16,0},... | collective-permute-start | bytes 98312 | tf_op jit(solution)/shard_map/ppermute | solution.py:23
  86.4 16.4 %copy-start = (f32[512,256]{0,1:T(8,128)S(1)}, f32[512,256]{0,1:T(8,128)}, u32[]{:S(2)}) copy-start(f32[512,256]{0,1:T(8,128)} %all-reduce.2.cloned.1.call-done) | copy-start | bytes 1572868
  87.8 16.5 %collective-permute-start.4 = (f32[64,256]{1,0:T(8,128)S(1)}, f32[64,256]{1,0:T(8,128)S(1)}, u32[]{:S(2)}, u32[]{:S(2)}) collective-permute-start(f32[64,256]{1,0:T(8,128)S(1)} %get-tuple-element.37), channel_id=1, source_target_pairs={{0,2},{2,0},{4,6},{6,4},{8,10},{10,8},{12,14},{14,12},{16,18},{18,... | collective-permute-start | bytes 196616 | tf_op jit(solution)/shard_map/ppermute | solution.py:31
  105.9 15.0 %collective-permute-start.5 = (f32[64,256]{1,0:T(8,128)S(1)}, f32[64,256]{1,0:T(8,128)S(1)}, u32[]{:S(2)}, u32[]{:S(2)}) collective-permute-start(f32[64,256]{1,0:T(8,128)S(1)} %get-tuple-element.23), channel_id=1, source_target_pairs={{0,4},{2,6},{4,0},{6,2},{8,12},{10,14},{12,8},{14,10},{16,20},{18,... | collective-permute-start | bytes 196616 | tf_op jit(solution)/shard_map/ppermute | solution.py:31
  122.6 15.1 %collective-permute-start.6 = (f32[64,256]{1,0:T(8,128)S(1)}, f32[64,256]{1,0:T(8,128)S(1)}, u32[]{:S(2)}, u32[]{:S(2)}) collective-permute-start(f32[64,256]{1,0:T(8,128)S(1)} %get-tuple-element.25), channel_id=1, source_target_pairs={{0,8},{2,10},{4,12},{6,14},{8,0},{10,2},{12,4},{14,6},{16,24},{18,... | collective-permute-start | bytes 196616 | tf_op jit(solution)/shard_map/ppermute | solution.py:31
  139.4 15.9 %collective-permute-start.7 = (f32[64,256]{1,0:T(8,128)S(1)}, f32[64,256]{1,0:T(8,128)S(1)}, u32[]{:S(2)}, u32[]{:S(2)}) collective-permute-start(f32[64,256]{1,0:T(8,128)S(1)} %get-tuple-element.27), channel_id=1, source_target_pairs={{0,16},{2,18},{4,20},{6,22},{8,24},{10,26},{12,28},{14,30},{16,0},... | collective-permute-start | bytes 196616 | tf_op jit(solution)/shard_map/ppermute | solution.py:31
Sparse Core Ops, SparseCore 0:
  70.7 14.4 all-reduce.1
